TPU v7x, 512 devices: a whole 4x4x16 slice. The times are simulated.
512 devices in a mesh: section: 2 (over y_lo), hid: 16 (over z), wid: 16 (over x, y_hi, core).
Axes of the slice: x: 4, y: 4 (y_hi: 2, y_lo: 2; y = y_hi * 2 + y_lo), z: 16, core: 2. Of those that a mesh axis runs over, the one named last changes fastest.
Arguments:
- weights: bfloat16 [2, 6144, 24576], P('section', 'hid', 'wid'), may hold values from -0.078125 to 0.078125
- preact: bfloat16 [1024, 24576], P(('section', 'hid'), 'wid'), may hold values from -6 to 6
- inputs: bfloat16 [1024, 6144], P(('section', 'wid'), 'hid'), may hold values from -6 to 6
- grad_out: bfloat16 [1024, 6144], P(('section', 'wid'), 'hid'), may hold values from -6 to 6
- row_state: float32 [2, 6144], P('section', 'hid'), may hold values from 32 to 256
- col_state: float32 [2, 24576], P('section', 'wid'), may hold values from 32 to 256
Outputs:
- input_grad: float32 [1024, 6144], P(('section', 'wid'), 'hid')
- update: float32 [2, 6144, 24576], P('section', 'hid', 'wid')
All inputs are finite; a program needn't handle non-finite values.
Results may differ from a plain program's by a relative error of at most 0.0029.
Values may be sent and summed in bfloat16 or wider, within the bound.
No kernel may reach another device: no remote copies, remote signals or barrier semaphores. Data moves between devices by JAX's collectives and lax.ppermute only.
A program may use at most 64 MiB of HBM per device.

v0:
```python
import jax
import jax.numpy as jnp
from jax import lax
from jax.sharding import PartitionSpec as P

D = 6144
FF = 24576
decay_rate = 0.9
root_half = 0.7071067811865476
inv_root_tau = 0.3989422804014327
LANES = 128


def normal_cdf(pre):
    return 0.5 * (1.0 + lax.erf(pre * root_half))


def gelu_value(pre):
    return pre * normal_cdf(pre)


def gelu_slope(pre):
    return normal_cdf(pre) + pre * jnp.exp(-0.5 * pre * pre) * inv_root_tau


def contract(left, right):
    return lax.dot_general(
        left, right, (((0,), (0,)), ((), ())), preferred_element_type=jnp.float32
    )


def exchange(blocks, axis):
    return lax.all_to_all(blocks, axis, split_axis=0, concat_axis=0, tiled=True)


def spread(block, axis):
    n = lax.axis_size(axis)
    copies = jnp.broadcast_to(block[None], (n,) + block.shape)
    return exchange(copies.reshape((n * block.shape[0],) + block.shape[1:]), axis)


def thirds(values, scalar):
    shape = (16, values.shape[0])
    row = lax.broadcasted_iota(jnp.int32, shape, 0)
    rest = jnp.where(row < 8, jnp.broadcast_to(values[None], shape), scalar)
    out = jnp.zeros(shape, jnp.float32)
    for k in range(3):
        term = lax.reduce_precision(rest, exponent_bits=8, mantissa_bits=7)
        out = jnp.where(row % 8 == k, term, out)
        rest = rest - term
    return out.astype(jnp.bfloat16)


def sum_blocks(partial, axis, groups):
    members = len(groups[0])
    columns = partial.shape[1]
    rows = partial.shape[0] // members
    power = jnp.clip(jnp.ceil(jnp.log2(jnp.maximum(jnp.max(jnp.abs(partial)), 1e-30))), -96.0, 96.0)
    coded = (partial * jnp.exp2(14.0 - power)).astype(jnp.float16).reshape(members, rows, columns)
    power = jnp.broadcast_to(power, (members, 8, columns)).astype(jnp.float16)
    taken = lax.all_to_all(
        jnp.concatenate([coded, power], axis=1),
        axis,
        split_axis=0,
        concat_axis=0,
        axis_index_groups=groups,
        tiled=True,
    )
    power = jnp.max(taken[:, rows:, :LANES].astype(jnp.float32), axis=(1, 2), keepdims=True)
    return jnp.sum(taken[:, :rows].astype(jnp.float32) * jnp.exp2(power - 14.0), axis=0)


def shards(weights, preact, inputs, grad_out, row_state, col_state):
    hid = lax.axis_size("hid")
    wid = lax.axis_size("wid")
    own_tile = weights[0]
    features, hidden = own_tile.shape
    half = hidden // 2
    rows = grad_out.shape[0]
    first = lax.axis_index("section") == 0
    even = lax.axis_index("hid") % 2 == 0
    home = lax.axis_index("section") == lax.axis_index("hid") % 2
    pair = ("section", "hid")

    def at(section, h):
        return section * hid + h

    over = [(at(h % 2, h), at(1 - h % 2, h)) for h in range(hid)]
    beside = [(at(h % 2, h ^ 1), at(h % 2, h)) for h in range(hid)]
    across = [(at(h % 2, h ^ 1), at(1 - h % 2, h)) for h in range(hid)]
    rings = [list(range(p, hid, 2)) for p in range(2)]

    def token_blocks(same, other):
        own = jnp.where(home, same, lax.ppermute(other, pair, over))
        near = lax.ppermute(same, pair, beside)
        far = lax.ppermute(other, pair, across)
        return (own, jnp.where(home, near, far))

    grad_pair = jnp.concatenate(token_blocks(grad_out, grad_out), axis=1)
    tile_near = lax.ppermute(
        own_tile[:, :half], pair, [(at(1, h), at(1, h ^ 1)) for h in range(hid)]
    )
    tile_over = lax.ppermute(own_tile[:, half:], pair, [(at(1, h), at(0, h)) for h in range(hid)])
    tile_far = lax.ppermute(
        own_tile[:, half:], pair, [(at(1, h), at(0, h ^ 1)) for h in range(hid)]
    )
    grad_half = spread(grad_pair, "wid")
    pre_own, pre_next = token_blocks(
        jnp.where(first, preact[:, half:], preact[:, :half]),
        jnp.where(first, preact[:, :half], preact[:, half:]),
    )
    grad_half, pre_own, pre_next = lax.optimization_barrier((grad_half, pre_own, pre_next))
    hidden_part = jnp.dot(
        grad_half[:, :features],
        jnp.where(first, tile_over, own_tile[:, :half]),
        preferred_element_type=jnp.float32,
    ) + jnp.dot(
        grad_half[:, features:],
        jnp.where(first, tile_far, tile_near),
        preferred_element_type=jnp.float32,
    )
    hidden_share = sum_blocks(hidden_part, "hid", rings)
    pre_half = jnp.concatenate(
        [jnp.where(even, pre_own, pre_next), jnp.where(even, pre_next, pre_own)]
    )
    pre_taken = lax.ppermute(pre_half, "section", [(0, 1)])
    act_share = gelu_value(
        jnp.concatenate([pre_half, pre_taken], axis=1).astype(jnp.float32)
    ).astype(jnp.bfloat16)
    pre_share = (hidden_share * gelu_slope(pre_half.astype(jnp.float32))).astype(jnp.bfloat16)
    pre_share = jnp.concatenate([lax.ppermute(pre_share, "section", [(1, 0)]), pre_share], axis=1)
    right = lax.all_gather(jnp.where(first, pre_share, act_share), "hid", axis=0, tiled=True)
    kept = jnp.where(first, inputs, grad_out)
    given = jnp.where(first, grad_out, inputs)
    taken = lax.ppermute(given, "section", [(0, 1), (1, 0)])
    left_own = jnp.concatenate([jnp.where(first, kept, taken), jnp.where(first, taken, kept)])
    left = jnp.swapaxes(
        spread(left_own, "wid").reshape(wid // 2, 2, 2, rows, features), 1, 2
    ).reshape(2 * wid * rows, features)
    gradient = contract(left, right)
    squares = gradient * gradient
    row_local = jnp.sum(squares, axis=1)
    col_local = jnp.sum(squares, axis=0)
    row_prev = row_state[0]
    col_prev = col_state[0]
    scalars = jnp.stack([jnp.sum(row_local), jnp.sum(row_prev)])
    tail = jnp.concatenate([scalars, jnp.zeros((4 * LANES - 2,), jnp.float32)])
    packed = jnp.concatenate([col_local, tail]).reshape(-1, LANES)
    over_hid = jnp.sum(spread(packed, "hid").reshape((hid,) + packed.shape), axis=0).reshape(-1)
    col_total = over_hid[:hidden]
    square_sum, prev_sum = (over_hid[hidden], over_hid[hidden + 1])
    partial = lax.dot_general(
        right, own_tile, (((1,), (1,)), ((), ())), preferred_element_type=jnp.float32
    ).astype(jnp.bfloat16)
    blocks = jnp.swapaxes(partial.reshape(wid // 2, 2, 2, rows, features), 1, 2)
    extra = thirds(row_local, square_sum)
    blocks = jnp.concatenate(
        [
            blocks.reshape(wid, 2 * rows, features),
            jnp.broadcast_to(extra[None], (wid,) + extra.shape),
        ],
        axis=1,
    )
    over_wid = jnp.sum(exchange(blocks, "wid").astype(jnp.float32), axis=0)
    input_sum = jnp.where(
        first, over_wid[:rows], lax.ppermute(over_wid[rows : 2 * rows], "section", [(0, 1)])
    )
    input_grad = input_sum + grad_out.astype(jnp.float32)
    row_total = jnp.sum(over_wid[2 * rows : 2 * rows + 8], axis=0)
    square_total = jnp.sum(over_wid[2 * rows + 8 :, 0])
    row_moment = decay_rate * row_prev + (1.0 - decay_rate) / FF * row_total
    col_moment = decay_rate * col_prev + (1.0 - decay_rate) / D * col_total
    row_mean = decay_rate / D * prev_sum + (1.0 - decay_rate) / FF / D * square_total
    update = gradient * lax.rsqrt(row_moment[:, None] * col_moment[None, :] / row_mean)
    return (input_grad, update[None])


def solution(mesh):
    placed = (
        P("section", "hid", "wid"),
        P(("section", "hid"), "wid"),
        P(("section", "wid"), "hid"),
        P(("section", "wid"), "hid"),
        P("section", "hid"),
        P("section", "wid"),
    )
    return jax.shard_map(
        shards,
        mesh=mesh,
        in_specs=placed,
        out_specs=(P(("section", "wid"), "hid"), P("section", "hid", "wid")),
        check_vma=False,
    )
```

profile of v0, /device:TPU:8, one launch (start us, length us, event | category | flops | bytes accessed | tf_op | source)
XLA Modules:
  0.0 273.0 jit_solution(15380726887972053118)
XLA Ops:
  7.2 1.4 collective-permute-start
  8.6 4.9 %collective-permute-start.1 = (bf16[32,384]{1,0:T(8,128)(2,1)}, bf16[32,384]{1,0:T(8,128)(2,1)S(1)}, u32[]{:S(2)}, u32[]{:S(2)}) collective-permute-start(bf16[32,384]{1,0:T(8,128)(2,1)} %param.9), channel_id=1, source_target_pairs={{16,0},{256,272},{48,32},{288,304},{80,64},{320,336},{112,96},{352... | collective-permute-start | bytes 73736 | tf_op jit(solution)/shard_map/ppermute | solution.py:95
  13.5 6.2 %collective-permute-start.2 = (bf16[32,384]{1,0:T(8,128)(2,1)}, bf16[32,384]{1,0:T(8,128)(2,1)S(1)}, u32[]{:S(2)}, u32[]{:S(2)}) collective-permute-start(bf16[32,384]{1,0:T(8,128)(2,1)} %param.9), channel_id=1, source_target_pairs={{16,256},{256,16},{48,288},{288,48},{80,320},{320,80},{112,352},{3... | collective-permute-start | bytes 73736 | tf_op jit(solution)/shard_map/ppermute | solution.py:96
  19.7 0.8 broadcast_select_fusion.10
  20.5 1.9 collective-permute-start.11
  22.4 1.3 fusion.28
  23.7 0.0 copy-start.2
  23.7 2.9 %collective-permute-start.7 = (bf16[384,768]{1,0:T(8,128)(2,1)S(1)}, bf16[384,768]{1,0:T(8,128)(2,1)}, u32[]{:S(2)}, u32[]{:S(2)}) collective-permute-start(bf16[384,768]{1,0:T(8,128)(2,1)S(1)} %get-tuple-element.16), channel_id=1, source_target_pairs={{256,16},{272,0},{288,48},{304,32},{320,80},{336,64},{352,112},{36... | collective-permute-start | bytes 1769480 | tf_op jit(solution)/shard_map/ppermute | solution.py:104
  26.6 5.3 %collective-permute-start.8 = (bf16[384,768]{1,0:T(8,128)(2,1)S(1)}, bf16[384,768]{1,0:T(8,128)(2,1)}, u32[]{:S(2)}, u32[]{:S(2)}) collective-permute-start(bf16[384,768]{1,0:T(8,128)(2,1)S(1)} %get-tuple-element.15), channel_id=1, source_target_pairs={{256,272},{272,256},{288,304},{304,288},{320,336},{336,320},{352,3... | collective-permute-start | bytes 1769480 | tf_op jit(solution)/shard_map/ppermute | solution.py:100
  32.0 0.6 broadcast_select_fusion.9
  32.7 1.0 broadcast_in_dim.22
  33.6 3.6 %all-to-all-start = ((bf16[16,32,768]{2,1,0:T(8,128)(2,1)}), bf16[16,32,768]{2,1,0:T(8,128)(2,1)S(1)}, u32[]{:S(2)}, u32[]{:S(2)}) async-start(bf16[16,32,768]{2,1,0:T(8,128)(2,1)} %broadcast_in_dim.22), calls=%async_computation | async-start | bytes 1572864 | tf_op jit(solution)/shard_map/all_to_all | solution.py:33
  37.3 1.4 collective-permute-start.3
  38.7 1.9 collective-permute-start.5
  40.7 4.1 %collective-permute-start.6 = (bf16[384,768]{1,0:T(8,128)(2,1)S(1)}, bf16[384,768]{1,0:T(8,128)(2,1)}, u32[]{:S(2)}, u32[]{:S(2)}) collective-permute-start(bf16[384,768]{1,0:T(8,128)(2,1)S(1)} %get-tuple-element.16), channel_id=1, source_target_pairs={{256,0},{272,16},{288,32},{304,48},{320,64},{336,80},{352,96},{368... | collective-permute-start | bytes 1769480 | tf_op jit(solution)/shard_map/ppermute | solution.py:103
  44.8 2.9 %collective-permute-done.3 = bf16[32,768]{1,0:T(8,128)(2,1)S(1)} collective-permute-done((bf16[32,768]{1,0:T(8,128)(2,1)S(1)}, bf16[32,768]{1,0:T(8,128)(2,1)S(1)}, u32[]{:S(2)}, u32[]{:S(2)}) %collective-permute-start.3) | collective-permute-done | bytes 49184 | tf_op jit(solution)/shard_map/ppermute | solution.py:94
  47.7 0.6 broadcast_select_fusion.5
  48.3 3.9 %collective-permute-start.4 = (bf16[32,768]{1,0:T(8,128)(2,1)S(1)}, bf16[32,768]{1,0:T(8,128)(2,1)S(1)}, u32[]{:S(2)}, u32[]{:S(2)}) collective-permute-start(bf16[32,768]{1,0:T(8,128)(2,1)S(1)} %get-tuple-element.14), channel_id=1, source_target_pairs={{16,0},{256,272},{48,32},{288,304},{80,64},{320,336},{112,96},{352... | collective-permute-start | bytes 147464 | tf_op jit(solution)/shard_map/ppermute | solution.py:95
  52.2 1.7 collective-permute-done.4
  54.0 0.6 broadcast_select_fusion.4
  54.6 1.6 fusion
  56.2 5.1 %collective-permute-done.6 = bf16[384,768]{1,0:T(8,128)(2,1)} collective-permute-done((bf16[384,768]{1,0:T(8,128)(2,1)S(1)}, bf16[384,768]{1,0:T(8,128)(2,1)}, u32[]{:S(2)}, u32[]{:S(2)}) %collective-permute-start.6) | collective-permute-done | bytes 589856 | tf_op jit(solution)/shard_map/ppermute | solution.py:103
  61.3 1.2 abs_reduce_fusion
  63.3 0.1 multiply_convert_fusion
  63.5 0.0 copy-start.6
  63.5 1.1 concatenate.25
  64.5 14.1 %all-to-all-start.1 = ((f16[8,72,768]{2,1,0:T(8,128)(2,1)}), f16[8,72,768]{2,1,0:T(8,128)(2,1)S(1)}, u32[]{:S(2)}, u32[]{:S(2)}) async-start(f16[8,72,768]{2,1,0:T(8,128)(2,1)} %concatenate.25), calls=%async_computation.1 | async-start | bytes 1769472 | tf_op jit(solution)/shard_map/all_to_all | solution.py:61
  78.6 0.0 all-gather.2.cloned.1.call-start
  78.7 1.3 collective-permute-start.10
  80.0 29.8 %all-to-all-done.1 = f16[8,72,768]{2,1,0:T(8,128)(2,1)S(1)} async-done(((f16[8,72,768]{2,1,0:T(8,128)(2,1)}), f16[8,72,768]{2,1,0:T(8,128)(2,1)S(1)}, u32[]{:S(2)}, u32[]{:S(2)}) %all-to-all-start.1) | async-done | bytes 884768 | tf_op jit(solution)/shard_map/all_to_all | solution.py:61
  109.8 0.1 convert_reduce_fusion.1
  110.0 0.2 multiply_reduce_fusion.3
  110.2 0.0 copy-start.11
  110.2 0.1 fusion.19
  110.4 5.6 %collective-permute-start.9 = (bf16[64,768]{1,0:T(8,128)(2,1)S(1)}, bf16[64,768]{1,0:T(8,128)(2,1)S(1)}, u32[]{:S(2)}, u32[]{:S(2)}) collective-permute-start(bf16[64,768]{1,0:T(8,128)(2,1)S(1)} %fusion.19), channel_id=1, source_target_pairs={{256,0},{257,1},{258,2},{259,3},{260,4},{261,5},{262,6},{263,7},{2... | collective-permute-start | bytes 294920 | tf_op jit(solution)/shard_map/ppermute | solution.py:131
  115.9 2.2 collective-permute-done.9
  118.1 0.8 fusion.11
  118.9 0.0 all-gather.2.cloned.1.call-update
  119.0 1.0 broadcast_in_dim.23
  119.9 5.8 %all-to-all-start.2 = ((bf16[16,64,384]{2,1,0:T(8,128)(2,1)}), bf16[16,64,384]{2,1,0:T(8,128)(2,1)S(1)}, u32[]{:S(2)}, u32[]{:S(2)}) async-start(bf16[16,64,384]{2,1,0:T(8,128)(2,1)} %broadcast_in_dim.23), calls=%async_computation.2 | async-start | bytes 1572864 | tf_op jit(solution)/shard_map/all_to_all | solution.py:33
  125.8 0.7 multiply_reduce_fusion.4
  126.5 14.4 %all-to-all-done.2 = bf16[16,64,384]{2,1,0:T(8,128)(2,1)S(1)} async-done(((bf16[16,64,384]{2,1,0:T(8,128)(2,1)}), bf16[16,64,384]{2,1,0:T(8,128)(2,1)S(1)}, u32[]{:S(2)}, u32[]{:S(2)}) %all-to-all-start.2) | async-done | bytes 786464 | tf_op jit(solution)/shard_map/all_to_all | solution.py:33
  140.9 0.1 copy.12
  141.0 63.7 %all-gather.2.cloned.1.call-done = bf16[1024,1536]{1,0:T(8,128)(2,1)} async-done(((bf16[64,1536]{1,0:T(8,128)(2,1)}), bf16[1024,1536]{1,0:T(8,128)(2,1)}) %all-gather.2.cloned.1.call-update) | async-done | bytes 3145744 | tf_op jit(solution)/shard_map/all_gather | solution.py:132
  204.8 5.4 %multiply_reduce_fusion.2 = (f32[384]{0:T(512)S(1)}, f32[1536]{0:T(1024)S(1)}, f32[]{:T(128)}, f32[384,1536]{1,0:T(8,128)}) fusion(bf16[1024,384]{1,0:T(8,128)(2,1)S(1)} %bitcast.38, bf16[1024,1536]{1,0:T(8,128)(2,1)} %all-gather.2.cloned.1.call-done), kind=kOutput, calls=%fused_computation.3 | convolution fusion | flops 1210316928 | bytes 6299140 | tf_op jit(solution)/shard_map/dot_general | solution.py:27
  210.1 1.4 concatenate.30
  211.5 0.7 broadcast_in_dim.27
  212.2 7.8 %all-to-all-start.3 = ((f32[16,16,128]{2,1,0:T(8,128)}), f32[16,16,128]{2,1,0:T(8,128)S(1)}, u32[]{:S(2)}, u32[]{:S(2)}) async-start(f32[16,16,128]{2,1,0:T(8,128)} %broadcast_in_dim.27), calls=%async_computation.3 | async-start | bytes 262144 | tf_op jit(solution)/shard_map/all_to_all | solution.py:33
  219.9 3.7 %convolution_convert_fusion = bf16[1024,384]{1,0:T(8,128)(2,1)S(1)} fusion(bf16[1024,1536]{1,0:T(8,128)(2,1)} %all-gather.2.cloned.1.call-done, bf16[1,384,1536]{2,1,0:T(8,128)(2,1)S(1)} %copy-done), kind=kOutput, calls=%fused_computation.9 | convolution fusion | flops 1208352768 | bytes 5111808 | tf_op jit(solution)/shard_map/dot_general | solution.py:152
  223.6 0.1 copy.11
  223.8 9.3 %all-to-all-done.3 = f32[16,16,128]{2,1,0:T(8,128)S(1)} async-done(((f32[16,16,128]{2,1,0:T(8,128)}), f32[16,16,128]{2,1,0:T(8,128)S(1)}, u32[]{:S(2)}, u32[]{:S(2)}) %all-to-all-start.3) | async-done | bytes 131104 | tf_op jit(solution)/shard_map/all_to_all | solution.py:33
  233.1 0.6 fusion.29
  233.6 0.7 fusion.23
  234.4 0.0 copy-start.10
  234.4 1.0 pad_maximum_fusion
  235.4 6.0 %all-to-all-start.4 = ((bf16[16,80,384]{2,1,0:T(8,128)(2,1)}), bf16[16,80,384]{2,1,0:T(8,128)(2,1)S(1)}, u32[]{:S(2)}, u32[]{:S(2)}) async-start(bf16[16,80,384]{2,1,0:T(8,128)(2,1)} %pad_maximum_fusion), calls=%async_computation.4 | async-start | bytes 1966080 | tf_op jit(solution)/shard_map/all_to_all | solution.py:33
  242.2 16.5 %all-to-all-done.4 = bf16[16,80,384]{2,1,0:T(8,128)(2,1)S(1)} async-done(((bf16[16,80,384]{2,1,0:T(8,128)(2,1)}), bf16[16,80,384]{2,1,0:T(8,128)(2,1)S(1)}, u32[]{:S(2)}, u32[]{:S(2)}) %all-to-all-start.4) | async-done | bytes 983072 | tf_op jit(solution)/shard_map/all_to_all | solution.py:33
  258.7 0.1 convert_reduce_fusion
  258.9 0.7 slice_reduce_fusion.1
  259.6 1.3 collective-permute-start.12
  261.5 0.0 copy-start.4
  261.5 1.8 multiply_bitcast_fusion
  263.3 2.2 collective-permute-done.12
  265.5 0.6 fusion.20
  (45 shorter events, 0.2 us)
Async XLA Ops:
  7.2 24.8 %copy-start.3 = (bf16[32,384]{1,0:T(8,128)(2,1)S(1)}, bf16[32,384]{1,0:T(8,128)(2,1)}, u32[]{:S(2)}) copy-start(bf16[32,384]{1,0:T(8,128)(2,1)} %param.9) | copy-start | bytes 73732
  7.2 24.8 %copy-start.7 = (bf16[32,384]{1,0:T(8,128)(2,1)S(1)}, bf16[32,384]{1,0:T(8,128)(2,1)}, u32[]{:S(2)}) copy-start(bf16[32,384]{1,0:T(8,128)(2,1)} %param.8) | copy-start | bytes 73732
  7.2 24.8 %collective-permute-start = (bf16[32,384]{1,0:T(8,128)(2,1)}, bf16[32,384]{1,0:T(8,128)(2,1)S(1)}, u32[]{:S(2)}, u32[]{:S(2)}) collective-permute-start(bf16[32,384]{1,0:T(8,128)(2,1)} %param.9), channel_id=1, source_target_pairs={{0,256},{272,16},{32,288},{304,48},{64,320},{336,80},{96,352},{368... | collective-permute-start | bytes 73736 | tf_op jit(solution)/shard_map/ppermute | solution.py:94
  8.6 24.0 %collective-permute-start.1 = (bf16[32,384]{1,0:T(8,128)(2,1)}, bf16[32,384]{1,0:T(8,128)(2,1)S(1)}, u32[]{:S(2)}, u32[]{:S(2)}) collective-permute-start(bf16[32,384]{1,0:T(8,128)(2,1)} %param.9), channel_id=1, source_target_pairs={{16,0},{256,272},{48,32},{288,304},{80,64},{320,336},{112,96},{352... | collective-permute-start | bytes 73736 | tf_op jit(solution)/shard_map/ppermute | solution.py:95
  13.5 19.1 %collective-permute-start.2 = (bf16[32,384]{1,0:T(8,128)(2,1)}, bf16[32,384]{1,0:T(8,128)(2,1)S(1)}, u32[]{:S(2)}, u32[]{:S(2)}) collective-permute-start(bf16[32,384]{1,0:T(8,128)(2,1)} %param.9), channel_id=1, source_target_pairs={{16,256},{256,16},{48,288},{288,48},{80,320},{320,80},{112,352},{3... | collective-permute-start | bytes 73736 | tf_op jit(solution)/shard_map/ppermute | solution.py:96
  20.5 6.2 %collective-permute-start.11 = (bf16[32,384]{1,0:T(8,128)(2,1)S(1)}, bf16[32,384]{1,0:T(8,128)(2,1)S(1)}, u32[]{:S(2)}, u32[]{:S(2)}) collective-permute-start(bf16[32,384]{1,0:T(8,128)(2,1)S(1)} %broadcast_select_fusion.10), channel_id=1, source_target_pairs={{0,256},{256,0},{1,257},{257,1},{2,258},{258,2},{3,259},{259,3},{4... | collective-permute-start | bytes 73736 | tf_op jit(solution)/shard_map/ppermute | solution.py:135
  23.7 13.5 %copy-start.2 = (bf16[32,1536]{1,0:T(8,128)(2,1)S(1)}, bf16[32,1536]{1,0:T(8,128)(2,1)}, u32[]{:S(2)}) copy-start(bf16[32,1536]{1,0:T(8,128)(2,1)} %param.7) | copy-start | bytes 294916
  23.7 30.8 %collective-permute-start.7 = (bf16[384,768]{1,0:T(8,128)(2,1)S(1)}, bf16[384,768]{1,0:T(8,128)(2,1)}, u32[]{:S(2)}, u32[]{:S(2)}) collective-permute-start(bf16[384,768]{1,0:T(8,128)(2,1)S(1)} %get-tuple-element.16), channel_id=1, source_target_pairs={{256,16},{272,0},{288,48},{304,32},{320,80},{336,64},{352,112},{36... | collective-permute-start | bytes 1769480 | tf_op jit(solution)/shard_map/ppermute | solution.py:104
  26.6 27.9 %collective-permute-start.8 = (bf16[384,768]{1,0:T(8,128)(2,1)S(1)}, bf16[384,768]{1,0:T(8,128)(2,1)}, u32[]{:S(2)}, u32[]{:S(2)}) collective-permute-start(bf16[384,768]{1,0:T(8,128)(2,1)S(1)} %get-tuple-element.15), channel_id=1, source_target_pairs={{256,272},{272,256},{288,304},{304,288},{320,336},{336,320},{352,3... | collective-permute-start | bytes 1769480 | tf_op jit(solution)/shard_map/ppermute | solution.py:100
  33.6 20.9 %all-to-all-start = ((bf16[16,32,768]{2,1,0:T(8,128)(2,1)}), bf16[16,32,768]{2,1,0:T(8,128)(2,1)S(1)}, u32[]{:S(2)}, u32[]{:S(2)}) async-start(bf16[16,32,768]{2,1,0:T(8,128)(2,1)} %broadcast_in_dim.22), calls=%async_computation | async-start | bytes 1572864 | tf_op jit(solution)/shard_map/all_to_all | solution.py:33
  37.3 24.1 %copy-start = (bf16[1,384,1536]{2,1,0:T(8,128)(2,1)S(1)}, bf16[1,384,1536]{2,1,0:T(8,128)(2,1)}, u32[]{:S(2)}) copy-start(bf16[1,384,1536]{2,1,0:T(8,128)(2,1)} %param.6) | copy-start | bytes 3538948
  37.3 10.4 %collective-permute-start.3 = (bf16[32,768]{1,0:T(8,128)(2,1)S(1)}, bf16[32,768]{1,0:T(8,128)(2,1)S(1)}, u32[]{:S(2)}, u32[]{:S(2)}) collective-permute-start(bf16[32,768]{1,0:T(8,128)(2,1)S(1)} %broadcast_select_fusion.2), channel_id=1, source_target_pairs={{0,256},{272,16},{32,288},{304,48},{64,320},{336,80},{96,352},{368... | collective-permute-start | bytes 147464 | tf_op jit(solution)/shard_map/ppermute | solution.py:94
  38.7 13.5 %collective-permute-start.5 = (bf16[32,768]{1,0:T(8,128)(2,1)S(1)}, bf16[32,768]{1,0:T(8,128)(2,1)S(1)}, u32[]{:S(2)}, u32[]{:S(2)}) collective-permute-start(bf16[32,768]{1,0:T(8,128)(2,1)S(1)} %broadcast_select_fusion.2), channel_id=1, source_target_pairs={{16,256},{256,16},{48,288},{288,48},{80,320},{320,80},{112,352},{3... | collective-permute-start | bytes 147464 | tf_op jit(solution)/shard_map/ppermute | solution.py:96
  40.7 20.7 %collective-permute-start.6 = (bf16[384,768]{1,0:T(8,128)(2,1)S(1)}, bf16[384,768]{1,0:T(8,128)(2,1)}, u32[]{:S(2)}, u32[]{:S(2)}) collective-permute-start(bf16[384,768]{1,0:T(8,128)(2,1)S(1)} %get-tuple-element.16), channel_id=1, source_target_pairs={{256,0},{272,16},{288,32},{304,48},{320,64},{336,80},{352,96},{368... | collective-permute-start | bytes 1769480 | tf_op jit(solution)/shard_map/ppermute | solution.py:103
  48.3 5.6 %collective-permute-start.4 = (bf16[32,768]{1,0:T(8,128)(2,1)S(1)}, bf16[32,768]{1,0:T(8,128)(2,1)S(1)}, u32[]{:S(2)}, u32[]{:S(2)}) collective-permute-start(bf16[32,768]{1,0:T(8,128)(2,1)S(1)} %get-tuple-element.14), channel_id=1, source_target_pairs={{16,0},{256,272},{48,32},{288,304},{80,64},{320,336},{112,96},{352... | collective-permute-start | bytes 147464 | tf_op jit(solution)/shard_map/ppermute | solution.py:95
  63.4 15.2 %copy-start.5 = (bf16[32,768]{1,0:T(8,128)(2,1)S(1)}, bf16[32,768]{1,0:T(8,128)(2,1)}, u32[]{:S(2)}) copy-start(bf16[32,768]{1,0:T(8,128)(2,1)} %broadcast_select_fusion.4) | copy-start | bytes 147460
  63.5 15.2 %copy-start.6 = (bf16[32,768]{1,0:T(8,128)(2,1)S(1)}, bf16[32,768]{1,0:T(8,128)(2,1)}, u32[]{:S(2)}) copy-start(bf16[32,768]{1,0:T(8,128)(2,1)} %get-tuple-element.6) | copy-start | bytes 147460
  64.5 54.4 %copy-start.8 = (bf16[32,384]{1,0:T(8,128)(2,1)S(1)}, bf16[32,384]{1,0:T(8,128)(2,1)}, u32[]{:S(2)}) copy-start(bf16[32,384]{1,0:T(8,128)(2,1)} %get-tuple-element.19) | copy-start | bytes 73732
  64.5 54.4 %copy-start.9 = (bf16[32,384]{1,0:T(8,128)(2,1)S(1)}, bf16[32,384]{1,0:T(8,128)(2,1)}, u32[]{:S(2)}) copy-start(bf16[32,384]{1,0:T(8,128)(2,1)} %get-tuple-element.20) | copy-start | bytes 73732
  64.5 45.3 %all-to-all-start.1 = ((f16[8,72,768]{2,1,0:T(8,128)(2,1)}), f16[8,72,768]{2,1,0:T(8,128)(2,1)S(1)}, u32[]{:S(2)}, u32[]{:S(2)}) async-start(f16[8,72,768]{2,1,0:T(8,128)(2,1)} %concatenate.25), calls=%async_computation.1 | async-start | bytes 1769472 | tf_op jit(solution)/shard_map/all_to_all | solution.py:61
  78.6 126.2 %all-gather.2.cloned.1.call-start = ((), (), s32[]{:S(2)}) async-start(), calls=%async_computation.5 | async-start | bytes 3342336 | tf_op jit(solution)/shard_map/all_gather | solution.py:132
  78.7 37.2 %collective-permute-start.10 = (bf16[64,768]{1,0:T(8,128)(2,1)S(1)}, bf16[64,768]{1,0:T(8,128)(2,1)S(1)}, u32[]{:S(2)}, u32[]{:S(2)}) collective-permute-start(bf16[64,768]{1,0:T(8,128)(2,1)S(1)} %pad_maximum_fusion.1), channel_id=1, source_target_pairs={{0,256},{1,257},{2,258},{3,259},{4,260},{5,261},{6,262},{7,263},{8... | collective-permute-start | bytes 294920 | tf_op jit(solution)/shard_map/ppermute | solution.py:126
  110.2 15.6 %copy-start.11 = (f32[1,384]{1,0:T(1,128)S(1)}, f32[1,384]{1,0:T(1,128)}, u32[]{:S(2)}) copy-start(f32[1,384]{1,0:T(1,128)} %param.10) | copy-start | bytes 4612
  110.4 7.8 %collective-permute-start.9 = (bf16[64,768]{1,0:T(8,128)(2,1)S(1)}, bf16[64,768]{1,0:T(8,128)(2,1)S(1)}, u32[]{:S(2)}, u32[]{:S(2)}) collective-permute-start(bf16[64,768]{1,0:T(8,128)(2,1)S(1)} %fusion.19), channel_id=1, source_target_pairs={{256,0},{257,1},{258,2},{259,3},{260,4},{261,5},{262,6},{263,7},{2... | collective-permute-start | bytes 294920 | tf_op jit(solution)/shard_map/ppermute | solution.py:131
  119.9 21.0 %all-to-all-start.2 = ((bf16[16,64,384]{2,1,0:T(8,128)(2,1)}), bf16[16,64,384]{2,1,0:T(8,128)(2,1)S(1)}, u32[]{:S(2)}, u32[]{:S(2)}) async-start(bf16[16,64,384]{2,1,0:T(8,128)(2,1)} %broadcast_in_dim.23), calls=%async_computation.2 | async-start | bytes 1572864 | tf_op jit(solution)/shard_map/all_to_all | solution.py:33
  212.2 20.9 %all-to-all-start.3 = ((f32[16,16,128]{2,1,0:T(8,128)}), f32[16,16,128]{2,1,0:T(8,128)S(1)}, u32[]{:S(2)}, u32[]{:S(2)}) async-start(f32[16,16,128]{2,1,0:T(8,128)} %broadcast_in_dim.27), calls=%async_computation.3 | async-start | bytes 262144 | tf_op jit(solution)/shard_map/all_to_all | solution.py:33
  234.4 7.8 %copy-start.10 = (f32[1,1536]{1,0:T(1,128)S(1)}, f32[1,1536]{1,0:T(1,128)}, u32[]{:S(2)}) copy-start(f32[1,1536]{1,0:T(1,128)} %param.11) | copy-start | bytes 18436
  235.4 26.1 %copy-start.1 = (f32[384,1536]{1,0:T(8,128)S(1)}, f32[384,1536]{1,0:T(8,128)}, u32[]{:S(2)}) copy-start(f32[384,1536]{1,0:T(8,128)} %get-tuple-element.26) | copy-start | bytes 7077892
  235.4 23.3 %all-to-all-start.4 = ((bf16[16,80,384]{2,1,0:T(8,128)(2,1)}), bf16[16,80,384]{2,1,0:T(8,128)(2,1)S(1)}, u32[]{:S(2)}, u32[]{:S(2)}) async-start(bf16[16,80,384]{2,1,0:T(8,128)(2,1)} %pad_maximum_fusion), calls=%async_computation.4 | async-start | bytes 1966080 | tf_op jit(solution)/shard_map/all_to_all | solution.py:33
  259.6 6.0 %collective-permute-start.12 = (f32[32,384]{1,0:T(8,128)S(1)}, f32[32,384]{1,0:T(8,128)S(1)}, u32[]{:S(2)}, u32[]{:S(2)}) collective-permute-start(f32[32,384]{1,0:T(8,128)S(1)} %slice.71), channel_id=1, source_target_pairs={{0,256},{1,257},{2,258},{3,259},{4,260},{5,261},{6,262},{7,263},{8... | collective-permute-start | bytes 147464 | tf_op jit(solution)/shard_map/ppermute | solution.py:166
  261.5 4.0 %copy-start.4 = (bf16[32,384]{1,0:T(8,128)(2,1)S(1)}, bf16[32,384]{1,0:T(8,128)(2,1)}, u32[]{:S(2)}) copy-start(bf16[32,384]{1,0:T(8,128)(2,1)} %param.9) | copy-start | bytes 73732
Sparse Core Ops, SparseCore 0:
  119.0 85.6 all-gather.1
where the time goes:
time: 274 us; the launch traced here: 273 us
  waiting for transfers between devices  148 us (54%)
  starting transfers between devices  79.5 us (29%)
  between operations  16.5 us (6%)
  matrix products  11.9 us (4%)
  other arithmetic  9.82 us (4%)
  local copies, waits for them, and re-layouts  7.24 us (3%)
    all_gather x1, waiting for transfers between devices, shards(): lax.all_gather(jnp.where(first, pre_share, act_share), 'hid', axis=0, til...  63.7 us
    all_to_all x4, waiting for transfers between devices, exchange(): return lax.all_to_all(blocks, axis, split_axis=0, concat_axis=0, tiled=True)  40.3 us
    all_to_all x1, waiting for transfers between devices, sum_blocks(): lax.all_to_all(jnp.concatenate([coded, power], axis=1), axis, split_axis=...  29.8 us
    all_to_all x4, starting transfers between devices, exchange(): return lax.all_to_all(blocks, axis, split_axis=0, concat_axis=0, tiled=True)  23.3 us
    all_to_all x1, starting transfers between devices, sum_blocks(): lax.all_to_all(jnp.concatenate([coded, power], axis=1), axis, split_axis=...  14.1 us
    ppermute x2, starting transfers between devices, token_blocks(): near = lax.ppermute(same, pair, beside)  8.77 us
    ppermute x2, starting transfers between devices, token_blocks(): far = lax.ppermute(other, pair, across)  8.11 us
    ppermute x1, starting transfers between devices, shards(): lax.ppermute(pre_share, 'section', [(1, 0)])  5.56 us
  transfers between devices with their start and end apart: 19, of which 10 were waited for; matrix products, arithmetic and copies ran while one was open for 5% of the time, Pallas kernels for 0%

commit v1 on v0

--- a/solution.py
+++ b/solution.py
@@ -129,7 +129,11 @@
     ).astype(jnp.bfloat16)
     pre_share = (hidden_share * gelu_slope(pre_half.astype(jnp.float32))).astype(jnp.bfloat16)
     pre_share = jnp.concatenate([lax.ppermute(pre_share, "section", [(1, 0)]), pre_share], axis=1)
-    right = lax.all_gather(jnp.where(first, pre_share, act_share), "hid", axis=0, tiled=True)
+    panel = jnp.where(first, pre_share, act_share)
+    state_next = lax.axis_size("hid")
+    after = jnp.stack(state_next * [panel], axis=0)
+    mat_out = lax.all_to_all(after, "hid", 0, 0)
+    right = jnp.concatenate(mat_out, axis=0)
     kept = jnp.where(first, inputs, grad_out)
     given = jnp.where(first, grad_out, inputs)
     taken = lax.ppermute(given, "section", [(0, 1), (1, 0)])

time: 274 us -> 349 us (1.27)
  the two profiles are of different devices: /device:TPU:8 before, /device:TPU:1 now
where the time goes in v1:
time: 349 us; the launch traced here: 348 us
  waiting for transfers between devices  216 us (62%)
  starting transfers between devices  97.7 us (28%)
  matrix products  11.6 us (3%)
  local copies, waits for them, and re-layouts  11.1 us (3%)
  other arithmetic  9.05 us (3%)
    all_to_all x1, waiting for transfers between devices, shards(): mat_out = lax.all_to_all(after, 'hid', 0, 0)  134 us
    all_to_all x4, starting transfers between devices, exchange(): return lax.all_to_all(blocks, axis, split_axis=0, concat_axis=0, tiled=True)  35.1 us
    all_to_all x1, waiting for transfers between devices, sum_blocks(): lax.all_to_all(jnp.concatenate([coded, power], axis=1), axis, split_axis=...  29.3 us
    all_to_all x4, waiting for transfers between devices, exchange(): return lax.all_to_all(blocks, axis, split_axis=0, concat_axis=0, tiled=True)  26.9 us
    all_to_all x1, starting transfers between devices, shards(): mat_out = lax.all_to_all(after, 'hid', 0, 0)  19.5 us
    all_to_all x1, starting transfers between devices, sum_blocks(): lax.all_to_all(jnp.concatenate([coded, power], axis=1), axis, split_axis=...  13.6 us
    ppermute x2, starting transfers between devices, token_blocks(): own = jnp.where(home, same, lax.ppermute(other, pair, over))  11.1 us
    ppermute x1, waiting for transfers between devices, shards(): lax.ppermute(pre_share, 'section', [(1, 0)])  9.03 us
  transfers between devices with their start and end apart: 19, of which 9 were waited for; matrix products, arithmetic and copies ran while one was open for 5% of the time, Pallas kernels for 0%

profile of v1, /device:TPU:1, one launch (start us, length us, event | category | flops | bytes accessed | tf_op | source)
XLA Modules:
  0.0 348.2 jit_solution(4691728486092756838)
XLA Ops:
  0.6 0.0 copy-start.4
  0.7 4.2 %collective-permute-start = (bf16[32,384]{1,0:T(8,128)(2,1)}, bf16[32,384]{1,0:T(8,128)(2,1)S(1)}, u32[]{:S(2)}, u32[]{:S(2)}) collective-permute-start(bf16[32,384]{1,0:T(8,128)(2,1)} %param.9), channel_id=1, source_target_pairs={{0,256},{272,16},{32,288},{304,48},{64,320},{336,80},{96,352},{368... | collective-permute-start | bytes 73736 | tf_op jit(solution)/shard_map/ppermute | solution.py:94
  4.8 1.3 collective-permute-start.1
  6.1 0.7 collective-permute-start.2
  6.8 0.8 broadcast_select_fusion.10
  7.5 6.4 %collective-permute-start.11 = (bf16[32,384]{1,0:T(8,128)(2,1)S(1)}, bf16[32,384]{1,0:T(8,128)(2,1)S(1)}, u32[]{:S(2)}, u32[]{:S(2)}) collective-permute-start(bf16[32,384]{1,0:T(8,128)(2,1)S(1)} %broadcast_select_fusion.10), channel_id=1, source_target_pairs={{0,256},{256,0},{1,257},{257,1},{2,258},{258,2},{3,259},{259,3},{4... | collective-permute-start | bytes 73736 | tf_op jit(solution)/shard_map/ppermute | solution.py:139
  14.0 1.3 fusion.28
  15.3 0.0 copy-start.3
  15.3 1.4 collective-permute-start.7
  16.8 1.5 collective-permute-start.8
  18.3 0.6 broadcast_select_fusion.9
  18.9 1.0 broadcast_in_dim.22
  19.9 8.4 %all-to-all-start = ((bf16[16,32,768]{2,1,0:T(8,128)(2,1)}), bf16[16,32,768]{2,1,0:T(8,128)(2,1)S(1)}, u32[]{:S(2)}, u32[]{:S(2)}) async-start(bf16[16,32,768]{2,1,0:T(8,128)(2,1)} %broadcast_in_dim.22), calls=%async_computation | async-start | bytes 1572864 | tf_op jit(solution)/shard_map/all_to_all | solution.py:33
  28.3 0.0 copy-start.1
  28.4 7.0 %collective-permute-start.3 = (bf16[32,768]{1,0:T(8,128)(2,1)S(1)}, bf16[32,768]{1,0:T(8,128)(2,1)S(1)}, u32[]{:S(2)}, u32[]{:S(2)}) collective-permute-start(bf16[32,768]{1,0:T(8,128)(2,1)S(1)} %broadcast_select_fusion.2), channel_id=1, source_target_pairs={{0,256},{272,16},{32,288},{304,48},{64,320},{336,80},{96,352},{368... | collective-permute-start | bytes 147464 | tf_op jit(solution)/shard_map/ppermute | solution.py:94
  35.4 0.7 collective-permute-start.5
  36.1 1.3 collective-permute-start.6
  37.4 3.7 %collective-permute-done.3 = bf16[32,768]{1,0:T(8,128)(2,1)S(1)} collective-permute-done((bf16[32,768]{1,0:T(8,128)(2,1)S(1)}, bf16[32,768]{1,0:T(8,128)(2,1)S(1)}, u32[]{:S(2)}, u32[]{:S(2)}) %collective-permute-start.3) | collective-permute-done | bytes 49184 | tf_op jit(solution)/shard_map/ppermute | solution.py:94
  41.0 0.6 broadcast_select_fusion.5
  41.7 1.3 collective-permute-start.4
  43.0 6.7 %collective-permute-done.4 = bf16[32,768]{1,0:T(8,128)(2,1)S(1)} collective-permute-done((bf16[32,768]{1,0:T(8,128)(2,1)S(1)}, bf16[32,768]{1,0:T(8,128)(2,1)S(1)}, u32[]{:S(2)}, u32[]{:S(2)}) %collective-permute-start.4) | collective-permute-done | bytes 49184 | tf_op jit(solution)/shard_map/ppermute | solution.py:95
  49.6 0.6 broadcast_select_fusion.4
  50.3 1.6 fusion
  51.9 5.9 %collective-permute-done.6 = bf16[384,768]{1,0:T(8,128)(2,1)} collective-permute-done((bf16[384,768]{1,0:T(8,128)(2,1)S(1)}, bf16[384,768]{1,0:T(8,128)(2,1)}, u32[]{:S(2)}, u32[]{:S(2)}) %collective-permute-start.6) | collective-permute-done | bytes 589856 | tf_op jit(solution)/shard_map/ppermute | solution.py:103
  57.9 2.3 abs_reduce_fusion
  60.9 0.1 multiply_convert_fusion
  61.1 0.0 copy-start.7
  61.1 1.1 concatenate.29
  62.1 13.6 %all-to-all-start.1 = ((f16[8,72,768]{2,1,0:T(8,128)(2,1)}), f16[8,72,768]{2,1,0:T(8,128)(2,1)S(1)}, u32[]{:S(2)}, u32[]{:S(2)}) async-start(f16[8,72,768]{2,1,0:T(8,128)(2,1)} %concatenate.29), calls=%async_computation.1 | async-start | bytes 1769472 | tf_op jit(solution)/shard_map/all_to_all | solution.py:61
  75.8 1.3 collective-permute-start.10
  77.1 29.3 %all-to-all-done.1 = f16[8,72,768]{2,1,0:T(8,128)(2,1)S(1)} async-done(((f16[8,72,768]{2,1,0:T(8,128)(2,1)}), f16[8,72,768]{2,1,0:T(8,128)(2,1)S(1)}, u32[]{:S(2)}, u32[]{:S(2)}) %all-to-all-start.1) | async-done | bytes 884768 | tf_op jit(solution)/shard_map/all_to_all | solution.py:61
  106.4 1.0 broadcast_in_dim.23
  107.4 7.8 %all-to-all-start.3 = ((bf16[16,64,384]{2,1,0:T(8,128)(2,1)}), bf16[16,64,384]{2,1,0:T(8,128)(2,1)S(1)}, u32[]{:S(2)}, u32[]{:S(2)}) async-start(bf16[16,64,384]{2,1,0:T(8,128)(2,1)} %broadcast_in_dim.23), calls=%async_computation.3 | async-start | bytes 1572864 | tf_op jit(solution)/shard_map/all_to_all | solution.py:33
  115.2 0.1 convert_reduce_fusion.1
  115.4 0.2 multiply_reduce_fusion.3
  115.6 0.1 fusion.19
  115.7 1.3 collective-permute-start.9
  117.0 9.0 %collective-permute-done.9 = bf16[64,768]{1,0:T(8,128)(2,1)S(1)} collective-permute-done((bf16[64,768]{1,0:T(8,128)(2,1)S(1)}, bf16[64,768]{1,0:T(8,128)(2,1)S(1)}, u32[]{:S(2)}, u32[]{:S(2)}) %collective-permute-start.9) | collective-permute-done | bytes 98336 | tf_op jit(solution)/shard_map/ppermute | solution.py:131
  126.1 0.1 fusion.11
  126.2 2.6 all-to-all-done.3
  128.8 1.9 stack.6
  130.7 19.5 %all-to-all-start.2 = ((bf16[16,64,1536]{2,1,0:T(8,128)(2,1)}), bf16[16,64,1536]{2,1,0:T(8,128)(2,1)S(1)}, u32[]{:S(2)}, u32[]{:S(2)}) async-start(bf16[16,64,1536]{2,1,0:T(8,128)(2,1)} %stack.6), calls=%async_computation.2 | async-start | bytes 6291456 | tf_op jit(solution)/shard_map/all_to_all | solution.py:135
  150.3 0.6 multiply_reduce_fusion.4
  150.9 2.1 copy.12
  153.0 134.1 %all-to-all-done.2 = bf16[16,64,1536]{2,1,0:T(8,128)(2,1)S(1)} async-done(((bf16[16,64,1536]{2,1,0:T(8,128)(2,1)}), bf16[16,64,1536]{2,1,0:T(8,128)(2,1)S(1)}, u32[]{:S(2)}, u32[]{:S(2)}) %all-to-all-start.2) | async-done | bytes 3145760 | tf_op jit(solution)/shard_map/all_to_all | solution.py:135
  287.1 4.6 %multiply_reduce_fusion.2 = (f32[384]{0:T(512)S(1)}, f32[1536]{0:T(1024)S(1)}, f32[]{:T(128)}, f32[384,1536]{1,0:T(8,128)}) fusion(bf16[1024,384]{1,0:T(8,128)(2,1)} %bitcast.41, bf16[1024,1536]{1,0:T(8,128)(2,1)S(1)} %bitcast.33), kind=kOutput, calls=%fused_computation.3 | convolution fusion | flops 1210316928 | bytes 6299140 | tf_op jit(solution)/shard_map/dot_general | solution.py:27
  291.8 1.3 concatenate.34
  293.0 0.7 broadcast_in_dim.27
  293.7 11.1 %all-to-all-start.4 = ((f32[16,16,128]{2,1,0:T(8,128)}), f32[16,16,128]{2,1,0:T(8,128)S(1)}, u32[]{:S(2)}, u32[]{:S(2)}) async-start(f32[16,16,128]{2,1,0:T(8,128)} %broadcast_in_dim.27), calls=%async_computation.4 | async-start | bytes 262144 | tf_op jit(solution)/shard_map/all_to_all | solution.py:33
  304.8 3.1 convolution_convert_fusion
  307.9 0.1 copy.11
  308.0 8.8 %all-to-all-done.4 = f32[16,16,128]{2,1,0:T(8,128)S(1)} async-done(((f32[16,16,128]{2,1,0:T(8,128)}), f32[16,16,128]{2,1,0:T(8,128)S(1)}, u32[]{:S(2)}, u32[]{:S(2)}) %all-to-all-start.4) | async-done | bytes 131104 | tf_op jit(solution)/shard_map/all_to_all | solution.py:33
  316.8 0.6 fusion.29
  317.4 0.7 fusion.23
  318.1 0.0 copy-start.11
  318.1 1.0 pad_maximum_fusion
  319.2 7.7 %all-to-all-start.5 = ((bf16[16,80,384]{2,1,0:T(8,128)(2,1)}), bf16[16,80,384]{2,1,0:T(8,128)(2,1)S(1)}, u32[]{:S(2)}, u32[]{:S(2)}) async-start(bf16[16,80,384]{2,1,0:T(8,128)(2,1)} %pad_maximum_fusion), calls=%async_computation.5 | async-start | bytes 1966080 | tf_op jit(solution)/shard_map/all_to_all | solution.py:33
  327.6 15.4 %all-to-all-done.5 = bf16[16,80,384]{2,1,0:T(8,128)(2,1)S(1)} async-done(((bf16[16,80,384]{2,1,0:T(8,128)(2,1)}), bf16[16,80,384]{2,1,0:T(8,128)(2,1)S(1)}, u32[]{:S(2)}, u32[]{:S(2)}) %all-to-all-start.5) | async-done | bytes 983072 | tf_op jit(solution)/shard_map/all_to_all | solution.py:33
  343.0 0.1 convert_reduce_fusion
  343.2 0.7 slice_reduce_fusion.1
  343.9 1.3 collective-permute-start.12
  345.8 0.0 copy-start.5
  345.8 1.8 multiply_bitcast_fusion
  347.6 0.6 fusion.20
  (47 shorter events, 0.2 us)
Async XLA Ops:
  0.6 17.6 %copy-start.4 = (bf16[32,384]{1,0:T(8,128)(2,1)S(1)}, bf16[32,384]{1,0:T(8,128)(2,1)}, u32[]{:S(2)}) copy-start(bf16[32,384]{1,0:T(8,128)(2,1)} %param.9) | copy-start | bytes 73732
  0.6 17.6 %copy-start.8 = (bf16[32,384]{1,0:T(8,128)(2,1)S(1)}, bf16[32,384]{1,0:T(8,128)(2,1)}, u32[]{:S(2)}) copy-start(bf16[32,384]{1,0:T(8,128)(2,1)} %param.8) | copy-start | bytes 73732
  0.7 17.6 %collective-permute-start = (bf16[32,384]{1,0:T(8,128)(2,1)}, bf16[32,384]{1,0:T(8,128)(2,1)S(1)}, u32[]{:S(2)}, u32[]{:S(2)}) collective-permute-start(bf16[32,384]{1,0:T(8,128)(2,1)} %param.9), channel_id=1, source_target_pairs={{0,256},{272,16},{32,288},{304,48},{64,320},{336,80},{96,352},{368... | collective-permute-start | bytes 73736 | tf_op jit(solution)/shard_map/ppermute | solution.py:94
  4.8 14.1 %collective-permute-start.1 = (bf16[32,384]{1,0:T(8,128)(2,1)}, bf16[32,384]{1,0:T(8,128)(2,1)S(1)}, u32[]{:S(2)}, u32[]{:S(2)}) collective-permute-start(bf16[32,384]{1,0:T(8,128)(2,1)} %param.9), channel_id=1, source_target_pairs={{16,0},{256,272},{48,32},{288,304},{80,64},{320,336},{112,96},{352... | collective-permute-start | bytes 73736 | tf_op jit(solution)/shard_map/ppermute | solution.py:95
  6.1 12.8 %collective-permute-start.2 = (bf16[32,384]{1,0:T(8,128)(2,1)}, bf16[32,384]{1,0:T(8,128)(2,1)S(1)}, u32[]{:S(2)}, u32[]{:S(2)}) collective-permute-start(bf16[32,384]{1,0:T(8,128)(2,1)} %param.9), channel_id=1, source_target_pairs={{16,256},{256,16},{48,288},{288,48},{80,320},{320,80},{112,352},{3... | collective-permute-start | bytes 73736 | tf_op jit(solution)/shard_map/ppermute | solution.py:96
  7.5 9.2 %collective-permute-start.11 = (bf16[32,384]{1,0:T(8,128)(2,1)S(1)}, bf16[32,384]{1,0:T(8,128)(2,1)S(1)}, u32[]{:S(2)}, u32[]{:S(2)}) collective-permute-start(bf16[32,384]{1,0:T(8,128)(2,1)S(1)} %broadcast_select_fusion.10), channel_id=1, source_target_pairs={{0,256},{256,0},{1,257},{257,1},{2,258},{258,2},{3,259},{259,3},{4... | collective-permute-start | bytes 73736 | tf_op jit(solution)/shard_map/ppermute | solution.py:139
  15.3 13.1 %copy-start.3 = (bf16[32,1536]{1,0:T(8,128)(2,1)S(1)}, bf16[32,1536]{1,0:T(8,128)(2,1)}, u32[]{:S(2)}) copy-start(bf16[32,1536]{1,0:T(8,128)(2,1)} %param.7) | copy-start | bytes 294916
  15.3 35.0 %collective-permute-start.7 = (bf16[384,768]{1,0:T(8,128)(2,1)S(1)}, bf16[384,768]{1,0:T(8,128)(2,1)}, u32[]{:S(2)}, u32[]{:S(2)}) collective-permute-start(bf16[384,768]{1,0:T(8,128)(2,1)S(1)} %get-tuple-element.16), channel_id=1, source_target_pairs={{256,16},{272,0},{288,48},{304,32},{320,80},{336,64},{352,112},{36... | collective-permute-start | bytes 1769480 | tf_op jit(solution)/shard_map/ppermute | solution.py:104
  16.8 33.5 %collective-permute-start.8 = (bf16[384,768]{1,0:T(8,128)(2,1)S(1)}, bf16[384,768]{1,0:T(8,128)(2,1)}, u32[]{:S(2)}, u32[]{:S(2)}) collective-permute-start(bf16[384,768]{1,0:T(8,128)(2,1)S(1)} %get-tuple-element.15), channel_id=1, source_target_pairs={{256,272},{272,256},{288,304},{304,288},{320,336},{336,320},{352,3... | collective-permute-start | bytes 1769480 | tf_op jit(solution)/shard_map/ppermute | solution.py:100
  19.9 30.4 %all-to-all-start = ((bf16[16,32,768]{2,1,0:T(8,128)(2,1)}), bf16[16,32,768]{2,1,0:T(8,128)(2,1)S(1)}, u32[]{:S(2)}, u32[]{:S(2)}) async-start(bf16[16,32,768]{2,1,0:T(8,128)(2,1)} %broadcast_in_dim.22), calls=%async_computation | async-start | bytes 1572864 | tf_op jit(solution)/shard_map/all_to_all | solution.py:33
  28.3 29.5 %copy-start.1 = (bf16[1,384,1536]{2,1,0:T(8,128)(2,1)S(1)}, bf16[1,384,1536]{2,1,0:T(8,128)(2,1)}, u32[]{:S(2)}) copy-start(bf16[1,384,1536]{2,1,0:T(8,128)(2,1)} %param.6) | copy-start | bytes 3538948
  28.4 12.6 %collective-permute-start.3 = (bf16[32,768]{1,0:T(8,128)(2,1)S(1)}, bf16[32,768]{1,0:T(8,128)(2,1)S(1)}, u32[]{:S(2)}, u32[]{:S(2)}) collective-permute-start(bf16[32,768]{1,0:T(8,128)(2,1)S(1)} %broadcast_select_fusion.2), channel_id=1, source_target_pairs={{0,256},{272,16},{32,288},{304,48},{64,320},{336,80},{96,352},{368... | collective-permute-start | bytes 147464 | tf_op jit(solution)/shard_map/ppermute | solution.py:94
  35.4 7.6 %collective-permute-start.5 = (bf16[32,768]{1,0:T(8,128)(2,1)S(1)}, bf16[32,768]{1,0:T(8,128)(2,1)S(1)}, u32[]{:S(2)}, u32[]{:S(2)}) collective-permute-start(bf16[32,768]{1,0:T(8,128)(2,1)S(1)} %broadcast_select_fusion.2), channel_id=1, source_target_pairs={{16,256},{256,16},{48,288},{288,48},{80,320},{320,80},{112,352},{3... | collective-permute-start | bytes 147464 | tf_op jit(solution)/shard_map/ppermute | solution.py:96
  36.1 21.8 %collective-permute-start.6 = (bf16[384,768]{1,0:T(8,128)(2,1)S(1)}, bf16[384,768]{1,0:T(8,128)(2,1)}, u32[]{:S(2)}, u32[]{:S(2)}) collective-permute-start(bf16[384,768]{1,0:T(8,128)(2,1)S(1)} %get-tuple-element.16), channel_id=1, source_target_pairs={{256,0},{272,16},{288,32},{304,48},{320,64},{336,80},{352,96},{368... | collective-permute-start | bytes 1769480 | tf_op jit(solution)/shard_map/ppermute | solution.py:103
  41.7 8.0 %collective-permute-start.4 = (bf16[32,768]{1,0:T(8,128)(2,1)S(1)}, bf16[32,768]{1,0:T(8,128)(2,1)S(1)}, u32[]{:S(2)}, u32[]{:S(2)}) collective-permute-start(bf16[32,768]{1,0:T(8,128)(2,1)S(1)} %get-tuple-element.14), channel_id=1, source_target_pairs={{16,0},{256,272},{48,32},{288,304},{80,64},{320,336},{112,96},{352... | collective-permute-start | bytes 147464 | tf_op jit(solution)/shard_map/ppermute | solution.py:95
  61.0 14.6 %copy-start.9 = (bf16[32,384]{1,0:T(8,128)(2,1)S(1)}, bf16[32,384]{1,0:T(8,128)(2,1)}, u32[]{:S(2)}) copy-start(bf16[32,384]{1,0:T(8,128)(2,1)} %get-tuple-element.19) | copy-start | bytes 73732
  61.0 14.6 %copy-start.10 = (bf16[32,384]{1,0:T(8,128)(2,1)S(1)}, bf16[32,384]{1,0:T(8,128)(2,1)}, u32[]{:S(2)}) copy-start(bf16[32,384]{1,0:T(8,128)(2,1)} %get-tuple-element.20) | copy-start | bytes 73732
  61.1 14.7 %copy-start.6 = (bf16[32,768]{1,0:T(8,128)(2,1)S(1)}, bf16[32,768]{1,0:T(8,128)(2,1)}, u32[]{:S(2)}) copy-start(bf16[32,768]{1,0:T(8,128)(2,1)} %broadcast_select_fusion.4) | copy-start | bytes 147460
  61.1 14.7 %copy-start.7 = (bf16[32,768]{1,0:T(8,128)(2,1)S(1)}, bf16[32,768]{1,0:T(8,128)(2,1)}, u32[]{:S(2)}) copy-start(bf16[32,768]{1,0:T(8,128)(2,1)} %get-tuple-element.6) | copy-start | bytes 147460
  62.1 44.3 %all-to-all-start.1 = ((f16[8,72,768]{2,1,0:T(8,128)(2,1)}), f16[8,72,768]{2,1,0:T(8,128)(2,1)S(1)}, u32[]{:S(2)}, u32[]{:S(2)}) async-start(f16[8,72,768]{2,1,0:T(8,128)(2,1)} %concatenate.29), calls=%async_computation.1 | async-start | bytes 1769472 | tf_op jit(solution)/shard_map/all_to_all | solution.py:61
  75.8 41.2 %collective-permute-start.10 = (bf16[64,768]{1,0:T(8,128)(2,1)S(1)}, bf16[64,768]{1,0:T(8,128)(2,1)S(1)}, u32[]{:S(2)}, u32[]{:S(2)}) collective-permute-start(bf16[64,768]{1,0:T(8,128)(2,1)S(1)} %pad_maximum_fusion.1), channel_id=1, source_target_pairs={{0,256},{1,257},{2,258},{3,259},{4,260},{5,261},{6,262},{7,263},{8... | collective-permute-start | bytes 294920 | tf_op jit(solution)/shard_map/ppermute | solution.py:126
  107.4 21.4 %all-to-all-start.3 = ((bf16[16,64,384]{2,1,0:T(8,128)(2,1)}), bf16[16,64,384]{2,1,0:T(8,128)(2,1)S(1)}, u32[]{:S(2)}, u32[]{:S(2)}) async-start(bf16[16,64,384]{2,1,0:T(8,128)(2,1)} %broadcast_in_dim.23), calls=%async_computation.3 | async-start | bytes 1572864 | tf_op jit(solution)/shard_map/all_to_all | solution.py:33
  115.7 10.3 %collective-permute-start.9 = (bf16[64,768]{1,0:T(8,128)(2,1)S(1)}, bf16[64,768]{1,0:T(8,128)(2,1)S(1)}, u32[]{:S(2)}, u32[]{:S(2)}) collective-permute-start(bf16[64,768]{1,0:T(8,128)(2,1)S(1)} %fusion.19), channel_id=1, source_target_pairs={{256,0},{257,1},{258,2},{259,3},{260,4},{261,5},{262,6},{263,7},{2... | collective-permute-start | bytes 294920 | tf_op jit(solution)/shard_map/ppermute | solution.py:131
  128.8 1.9 copy-start
  130.7 19.6 %copy-start.12 = (f32[1,384]{1,0:T(1,128)S(1)}, f32[1,384]{1,0:T(1,128)}, u32[]{:S(2)}) copy-start(f32[1,384]{1,0:T(1,128)} %param.10) | copy-start | bytes 4612
  130.7 156.4 %all-to-all-start.2 = ((bf16[16,64,1536]{2,1,0:T(8,128)(2,1)}), bf16[16,64,1536]{2,1,0:T(8,128)(2,1)S(1)}, u32[]{:S(2)}, u32[]{:S(2)}) async-start(bf16[16,64,1536]{2,1,0:T(8,128)(2,1)} %stack.6), calls=%async_computation.2 | async-start | bytes 6291456 | tf_op jit(solution)/shard_map/all_to_all | solution.py:135
  293.7 23.1 %all-to-all-start.4 = ((f32[16,16,128]{2,1,0:T(8,128)}), f32[16,16,128]{2,1,0:T(8,128)S(1)}, u32[]{:S(2)}, u32[]{:S(2)}) async-start(f32[16,16,128]{2,1,0:T(8,128)} %broadcast_in_dim.27), calls=%async_computation.4 | async-start | bytes 262144 | tf_op jit(solution)/shard_map/all_to_all | solution.py:33
  318.1 9.5 %copy-start.11 = (f32[1,1536]{1,0:T(1,128)S(1)}, f32[1,1536]{1,0:T(1,128)}, u32[]{:S(2)}) copy-start(f32[1,1536]{1,0:T(1,128)} %param.11) | copy-start | bytes 18436
  319.2 26.6 %copy-start.2 = (f32[384,1536]{1,0:T(8,128)S(1)}, f32[384,1536]{1,0:T(8,128)}, u32[]{:S(2)}) copy-start(f32[384,1536]{1,0:T(8,128)} %get-tuple-element.26) | copy-start | bytes 7077892
  319.2 23.9 %all-to-all-start.5 = ((bf16[16,80,384]{2,1,0:T(8,128)(2,1)}), bf16[16,80,384]{2,1,0:T(8,128)(2,1)S(1)}, u32[]{:S(2)}, u32[]{:S(2)}) async-start(bf16[16,80,384]{2,1,0:T(8,128)(2,1)} %pad_maximum_fusion), calls=%async_computation.5 | async-start | bytes 1966080 | tf_op jit(solution)/shard_map/all_to_all | solution.py:33
  343.9 3.8 %collective-permute-start.12 = (f32[32,384]{1,0:T(8,128)S(1)}, f32[32,384]{1,0:T(8,128)S(1)}, u32[]{:S(2)}, u32[]{:S(2)}) collective-permute-start(f32[32,384]{1,0:T(8,128)S(1)} %slice.71), channel_id=1, source_target_pairs={{0,256},{1,257},{2,258},{3,259},{4,260},{5,261},{6,262},{7,263},{8... | collective-permute-start | bytes 147464 | tf_op jit(solution)/shard_map/ppermute | solution.py:170
  345.8 1.8 copy-start.5
